TPU v7x, 512 devices: a whole 4x8x8 slice. The times are simulated.
512 devices in a mesh: stream: 4 (over z_lo), span: 8 (over z_hi, x), wall: 16 (over y, core).
Axes of the slice: x: 4, y: 8, z: 8 (z_hi: 2, z_lo: 4; z = z_hi * 4 + z_lo), core: 2. Of those that a mesh axis runs over, the one named last changes fastest.
Arguments:
- adj_init: float32 [17, 48, 128, 1024], P(None, 'stream', 'wall', 'span'), may hold values from -1.2 to 1.2
- adj_source: float32 [17, 48, 128, 1024], P(None, 'stream', 'wall', 'span'), may hold values from -12 to 12
- velocity: float32 [3, 48, 128, 1024], P(None, 'stream', 'wall', 'span'), may hold values from -4 to 4
- sound: float32 [48, 128, 1024], P('stream', 'wall', 'span'), may hold values from 0.5 to 2
- face_couple: float32 [3, 2, 17, 17], replicated, may hold values from -0.36 to 0.36
- precond_inv: float32 [17, 17], replicated, may hold values from -0.3 to 1.3
- wall_code: int32 [48, 1024], replicated, may hold values from 0 to 3
- spall_mask: int32 [48, 1024], replicated, may hold values 0 or 1
- wall_table: float32 [4, 17], replicated, may hold values from 0.5 to 2
- spall_gain: float32 [17], replicated, may hold values from 0.5 to 3
Outputs:
- adjoint_out: float32 [17, 48, 128, 1024], P(None, 'stream', 'wall', 'span')
- residual_out: float32 [17, 48, 128, 1024], P(None, 'stream', 'wall', 'span')
All inputs are finite; a program needn't handle non-finite values.
Results may differ from a plain program's by a relative error of at most 0.00015.
Values sent between devices are 32-bit elements; how exact they have to be, the bound alone decides.
A program may use at most 128 MiB of HBM per device.

v0:
```python
import jax
import jax.numpy as jnp
from jax import lax
from jax.experimental import pallas as pl
from jax.experimental.pallas import tpu as pltpu
from jax.sharding import PartitionSpec as P

NV = 17
X = 12
WL = 8
L = 128
B1 = 144
ROWS = NV * WL
PAIRS = X // 2
R1, R0, R2 = 17, 18, 19
WROWS = 18 * X
F32, BF = jnp.float32, jnp.bfloat16
HI = lax.Precision.HIGHEST
MESH = pl.DeviceIdType.MESH


def iota(shape, dim):
    return lax.broadcasted_iota(jnp.int32, shape, dim)


def dot(a, b):
    return lax.dot_general(a, b, (((1,), (0,)), ((), ())), preferred_element_type=F32)


def dot_nt(a, b):
    return lax.dot_general(a, b, (((1,), (1,)), ((), ())), preferred_element_type=F32)


def split(v):
    hi = v.astype(BF)
    return hi, (v - hi.astype(F32)).astype(BF)


def stacked(hi, lo, rows):
    parts = [hi, lo, hi]
    short = rows - 3 * hi.shape[0]
    return jnp.concatenate(parts + [jnp.zeros((short, hi.shape[1]), BF)], axis=0)


def hi_lo(weights, from_lo):
    hi = weights.astype(BF).astype(F32)
    return jnp.where(from_lo, weights - hi, hi).astype(BF)


def build_weights(fc, pinv, w_all, w_p, w_span, w_wall):
    spread = (iota((B1, NV), 0) // WL == iota((B1, NV), 1)).astype(F32)

    def rows_of(couple):
        return lax.dot_general(spread, couple, (((1,), (1,)), ((), ())), precision=HI, preferred_element_type=F32)

    k = iota((B1, 512), 1)
    kk = jnp.where(k >= 2 * B1, k - 2 * B1, jnp.where(k >= B1, k - B1, k))
    used = k < 3 * B1
    kj = iota((2 * NV, 512), 1)
    kj = jnp.where(kj >= 2 * B1, kj - 2 * B1, jnp.where(kj >= B1, kj - B1, kj))
    js = iota((2 * NV, 512), 0)
    lanes = [((kj // WL == js // 2) & (js % 2 == s)).astype(F32) for s in range(2)]
    p_lanes = (kj[:NV] // WL == js[:NV]).astype(F32)
    w = iota((B1, 512), 0) % WL
    wk = kk % WL

    def expand(rows, lanes, shift):
        full = lax.dot_general(rows, lanes, (((1,), (0,)), ((), ())), precision=HI, preferred_element_type=F32)
        full = jnp.where(used & (wk == w + shift), full, 0.0)
        hi = full.astype(BF).astype(F32)
        return jnp.where(k >= 2 * B1, full - hi, hi)

    rows = [rows_of(fc[d].reshape(2 * NV, NV)) for d in range(3)]
    for d in range(3):
        shifts = (-1, 1) if d == 1 else (0, 0)
        both = [expand(rows[d], lanes[s], shifts[s])[:ROWS] for s in range(2)]
        w_all[2 * ROWS * d : 2 * ROWS * (d + 1), :] = jnp.concatenate(both, axis=0).astype(BF)
    p_rows = lax.dot_general(spread, pinv[...], (((1,), (0,)), ((), ())), precision=HI, preferred_element_type=F32)
    w_p[...] = expand(p_rows, p_lanes, 0).astype(BF)

    ks = iota((B1, 256), 1)
    rs = iota((B1, 256), 0)
    js = iota((2 * NV, 256), 0)
    kj = iota((2 * NV, 256), 1)
    for s in range(2):
        s_lanes = ((kj // WL == js // 2) & (js % 2 == s)).astype(F32)
        full = lax.dot_general(rows[2], s_lanes, (((1,), (0,)), ((), ())), precision=HI, preferred_element_type=F32)
        full = jnp.where((rs % WL == ks % WL) & (ks < ROWS), full, 0.0)
        full = jnp.where((rs >= ROWS) & (rs == ks), 1.0, full)
        hi = full.astype(BF)
        lo = (full - hi.astype(F32)).astype(BF)
        w_span[:, 768 * s : 768 * s + 256] = hi
        w_span[:, 768 * s + 256 : 768 * s + 512] = hi
        w_span[:, 768 * s + 512 : 768 * s + 768] = lo

    def mod48(v):
        return jnp.where(v >= 96, v - 96, jnp.where(v >= 48, v - 48, v))

    kw = mod48(ks)
    kv = mod48(kj)
    full = 0.0
    for s in range(2):
        pick = ((kv - 24 * s == js // 2) & (js % 2 == s)).astype(F32)
        part = lax.dot_general(rows[1], pick, (((1,), (0,)), ((), ())), precision=HI, preferred_element_type=F32)
        full = full + jnp.where(rs % WL == (WL - 1) * s, part, 0.0)
    full = jnp.where((ks < 144) & (rs < ROWS), full, 0.0)
    w_wall[...] = hi_lo(full, ks >= 96)


def kernel(
    adj_in, src_in, vel_in, snd_in, code_in, mask_in, fc_in, pinv_in, table_in, gain_in,
    adj_out, res_out,
    ar, src, vel, snd, code, mask, fc, pinv, table, gain, res, split_a, g_buf, diag,
    w_all, w_p, w_span, w_wall, take, tg,
    send_s, send_w, send_p, recv_s, recv_w, recv_p, spread, rates,
    in_sem, send_sem, recv_sem,
):
    st, sp, wl = (lax.axis_index(a) for a in ("stream", "span", "wall"))
    n_st, n_sp, n_wl = (lax.axis_size(a) for a in ("stream", "span", "wall"))
    right, left = lax.rem(sp + 1, n_sp), lax.rem(sp + n_sp - 1, n_sp)
    ways = [
        ({"stream": st + 1}, st < n_st - 1, st > 0),
        ({"stream": st - 1}, st > 0, st < n_st - 1),
        ({"wall": wl + 1}, wl < n_wl - 1, wl > 0),
        ({"wall": wl - 1}, wl > 0, wl < n_wl - 1),
        ({"span": right}, None, None),
        ({"span": left}, None, None),
    ]

    def when(cond, fn):
        if cond is None:
            fn()
        else:
            pl.when(cond)(fn)

    barrier = pltpu.get_barrier_semaphore()
    for device, sends, _ in ways:
        when(sends, lambda device=device: pl.semaphore_signal(barrier, inc=1, device_id=device, device_id_type=MESH))

    loads = [
        pltpu.make_async_copy(adj_in, ar.at[0 : NV * X * WL, :], in_sem.at[0]),
        pltpu.make_async_copy(vel_in, vel, in_sem.at[1]),
        pltpu.make_async_copy(snd_in, snd, in_sem.at[2]),
        pltpu.make_async_copy(src_in, src, in_sem.at[3]),
    ]
    small = [
        pltpu.make_async_copy(fc_in, fc, in_sem.at[6]),
        pltpu.make_async_copy(pinv_in, pinv, in_sem.at[7]),
        pltpu.make_async_copy(table_in, table, in_sem.at[8]),
        pltpu.make_async_copy(gain_in, gain, in_sem.at[9]),
    ]
    for c in small + loads:
        c.start()
    row0 = pl.multiple_of(X * st - 4 * lax.rem(st, 2), 8)
    off = 4 * lax.rem(st, 2)
    col0 = pl.multiple_of(L * sp, L)
    at_wall = wl == 0
    code_loads = [
        pltpu.make_async_copy(code_in.at[pl.ds(row0, 16), pl.ds(col0, L)], code, in_sem.at[4]),
        pltpu.make_async_copy(mask_in.at[pl.ds(row0, 16), pl.ds(col0, L)], mask, in_sem.at[5]),
    ]

    @pl.when(at_wall)
    def _():
        for c in code_loads:
            c.start()

    for r in range(2):
        for side in range(2):
            recv_w[r, side, WROWS:, :] = jnp.zeros((recv_w.shape[2] - WROWS, L), F32)
            spread[side] = jnp.zeros((2, 32, L), F32)
            send_p[r, side] = jnp.zeros((2, 16, L), F32)

            @pl.when(jnp.logical_not(ways[side][2]))
            def _():
                recv_s[r, side] = jnp.zeros((18, WL, L), F32)

            @pl.when(jnp.logical_not(ways[2 + side][2]))
            def _():
                recv_w[r, side, 0:WROWS, :] = jnp.zeros((WROWS, L), F32)

    g_buf[0, 0:ROWS, :] = jnp.zeros((ROWS, 2 * L), F32)
    g_buf[PAIRS + 1, ROWS : 2 * ROWS, :] = jnp.zeros((ROWS, 2 * L), F32)
    t_row, t_col = iota((32, 256 * X), 0), iota((32, 256 * X), 1)
    take_at = jnp.where(t_row < 16, L - 1, 0) + L * lax.rem(t_col // L, 2)
    take[...] = ((t_col // 256 == t_row % 16) & (t_col % 256 == take_at)).astype(BF)
    for c in small:
        c.wait()
    build_weights(fc, pinv, w_all, w_p, w_span, w_wall)

    for c in loads[:3]:
        c.wait()
    for d, slot in ((0, R0), (1, R1), (2, R2)):
        ar[slot * X * WL : (slot + 1) * X * WL, :] = (jnp.abs(vel[d]) + snd[...]).reshape(X * WL, L)

    def at(slot, x):
        start = slot * X * WL + x * WL
        return pl.ds(start if isinstance(start, int) else pl.multiple_of(start, WL), WL)

    def one(slot, x):
        return ar[at(slot, x), :]

    def plane(x):
        return jnp.concatenate([one(j, x) for j in range(NV)], axis=0)

    def plane3(x):
        return plane(x).reshape(NV, WL, L)

    def store_split(x, value):
        hi, lo = split(jnp.concatenate([value, one(R2, x)], axis=0))
        split_a[x, 0] = hi
        split_a[x, 1] = lo

    def first_split(x, _):
        store_split(x, plane(x))
        return 0

    lax.fori_loop(0, X, first_split, 0)

    def copies(r):
        out = []
        for n, (device, _, _) in enumerate(ways):
            bufs = ((send_s, recv_s), (send_w, recv_w), (send_p, recv_p))[n // 2]
            side = n % 2
            if n // 2 == 1:
                dst = bufs[1].at[r, side, 0:WROWS, :]
            else:
                dst = bufs[1].at[r, side]
            out.append(
                pltpu.make_async_remote_copy(
                    src_ref=bufs[0].at[r, side],
                    dst_ref=dst,
                    send_sem=send_sem.at[r, n],
                    recv_sem=recv_sem.at[r, n],
                    device_id=device,
                    device_id_type=MESH,
                )
            )
        return out

    def pack(r):
        faces = jnp.concatenate([split_a[x, h] for x in range(X) for h in range(2)], axis=1)
        both = dot_nt(take[...], faces)
        for side in range(2):
            send_p[r, side, 0] = both[16 * side : 16 * side + 16, 0:L]
            send_p[r, side, 1, :, 0 : B1 - L] = both[16 * side : 16 * side + 16, L:B1]
        for side, w in ((0, WL - 1), (1, 0)):
            send_w[r, side] = ar[pl.ds(w, WROWS, stride=WL), :]
        for side, x in ((0, X - 1), (1, 0)):
            send_s[r, side, 0:NV] = plane3(x)
            send_s[r, side, NV] = one(R0, x)

    def send(r):
        for n, c in enumerate(copies(r)):
            when(ways[n][1], c.start)

    def receive(r):
        for n, c in enumerate(copies(r)):
            when(ways[n][2], c.wait_recv)

    lane = iota((WL, L), 1)
    sub = iota((WL, L), 0)

    def planes_rhs(hi_lo_pairs):
        return jnp.concatenate([stacked(h, l, 512) for h, l in hi_lo_pairs], axis=1)

    def local():
        def couple(p, _):
            rhs = planes_rhs([(split_a[2 * p + q, 0], split_a[2 * p + q, 1]) for q in range(2)])
            g_buf[p + 1] = dot(w_all[...], rhs)
            return 0

        lax.fori_loop(0, PAIRS, couple, 0)

        def gather(p, _):
            for q in range(2):
                x = 2 * p + q
                here = slice(q * L, (q + 1) * L)
                r0, r1, r2 = one(R0, x), one(R1, x), one(R2, x)
                m00 = 0.5 * (r0 + one(R0, jnp.maximum(x - 1, 0)))
                m01 = 0.5 * (r0 + one(R0, jnp.minimum(x + 1, X - 1)))
                m10 = 0.5 * (r1 + pltpu.roll(r1, 1, 0))
                m11 = 0.5 * (r1 + pltpu.roll(r1, WL - 1, 0))
                m20 = jnp.where(lane == 0, 0.0, 0.5 * (r2 + pltpu.roll(r2, 1, 1)))
                m21 = jnp.where(lane == L - 1, 0.0, 0.5 * (r2 + pltpu.roll(r2, L - 1, 1)))

                def g(page, n, part):
                    return g_buf[page, n * ROWS : (n + 1) * ROWS, part]

                lower, upper = slice(0, L), slice(L, 2 * L)
                g00 = g(p + 1, 0, lower) if q == 1 else g(p, 0, upper)
                g01 = g(p + 2, 1, lower) if q == 1 else g(p + 1, 1, upper)
                terms = [
                    (m00, g00),
                    (m01, g01),
                    (m10, g(p + 1, 2, here)),
                    (m11, g(p + 1, 3, here)),
                    (m20, pltpu.roll(g(p + 1, 4, here), 1, 1)),
                    (m21, pltpu.roll(g(p + 1, 5, here), L - 1, 1)),
                ]
                total = src[:, x]
                for m, v in terms:
                    total = total - m[None] * v.reshape(NV, WL, L)
                res[:, x] = total
            return 0

        lax.fori_loop(0, PAIRS, gather, 0)

        @pl.when(at_wall)
        def _():
            def wall_term(x, _):
                res[:, x] = res[:, x] - diag[:, x] * plane3(x)
                return 0

            lax.fori_loop(0, X, wall_term, 0)

    def finish(r, last):
        for side in range(2):
            for half in range(2):
                spread[side, half, pl.ds(2 - side, X, stride=2), :] = recv_p[r, side, half, 0:X, :]
        cols = []
        for side in range(2):
            hi, lo = split(jnp.concatenate([spread[side, 0], spread[side, 1]], axis=1))
            cols += [hi, lo, hi]
        cols = jnp.concatenate(cols, axis=1)
        cols = jnp.concatenate([cols, jnp.zeros((L - 32, cols.shape[1]), BF)], axis=0)
        edge_cols = dot_nt(w_span[...], cols)

        ends = [split(recv_s[r, side].reshape(B1, L)) for side in range(2)]
        g_ends = dot(w_all[0 : 2 * ROWS, :], planes_rhs(ends))
        for side, x in ((0, 0), (1, X - 1)):
            rate = 0.5 * (one(R0, x) + recv_s[r, side, NV])
            g_end = g_ends[side * ROWS : (side + 1) * ROWS, side * L : (side + 1) * L]
            res[:, x] = res[:, x] - rate[None] * g_end.reshape(NV, WL, L)

        for p in range(PAIRS):
            xs = (2 * p, 2 * p + 1)
            rhs = []
            for x in xs:
                rows = jnp.concatenate([recv_w[r, side, pl.ds(x, 24, stride=X), :] for side in range(2)], axis=0)
                rhs.append(stacked(*split(rows), 256))
            g_wall = dot(w_wall[...], jnp.concatenate(rhs, axis=1))
            parts = []
            for q, x in enumerate(xs):
                edge = pltpu.roll(edge_cols, (2 * L - 2 * x - 2) % L, 1)
                if r == 0:
                    r0, r1, r2 = one(R0, x), one(R1, x), one(R2, x)
                    r0m = recv_s[r, 0, NV] if x == 0 else one(R0, x - 1)
                    r0p = recv_s[r, 1, NV] if x == X - 1 else one(R0, x + 1)
                    low = recv_w[r, 0, NV * X + x : NV * X + x + 1, :]
                    high = recv_w[r, 1, NV * X + x : NV * X + x + 1, :]
                    r1m = jnp.where(sub == 0, jnp.broadcast_to(low, (WL, L)), pltpu.roll(r1, 1, 0))
                    r1p = jnp.where(sub == WL - 1, jnp.broadcast_to(high, (WL, L)), pltpu.roll(r1, WL - 1, 0))
                    beyond = edge[ROWS:B1]
                    r2m = jnp.where(lane == 0, beyond, pltpu.roll(r2, 1, 1))
                    r2p = jnp.where(lane == L - 1, beyond, pltpu.roll(r2, L - 1, 1))
                    total = 1.0 + (r0 + r1 + r2) + 0.5 * ((r0m + r0p) + (r1m + r1p) + (r2m + r2p))
                    rate_w = jnp.where(sub == 0, 0.5 * (r1 + r1m), jnp.where(sub == WL - 1, 0.5 * (r1 + r1p), 0.0))
                    rate_s = jnp.where(lane == 0, 0.5 * (r2 + r2m), jnp.where(lane == L - 1, 0.5 * (r2 + r2p), 0.0))
                    rates[x, 0] = total
                    rates[x, 1] = 1.0 / total
                    rates[x, 2] = rate_w
                    rates[x, 3] = rate_s
                total, rate_w, rate_s = rates[x, 0], rates[x, 2], rates[x, 3]
                value = res[:, x] - total[None] * plane3(x)
                value = value - rate_w[None] * g_wall[0:ROWS, q * L : (q + 1) * L].reshape(NV, WL, L)
                value = value - rate_s[None] * edge[0:ROWS].reshape(NV, WL, L)
                if last:
                    res_out[:, x] = value
                value = jnp.concatenate([value.reshape(ROWS, L), jnp.zeros((WL, L), F32)], axis=0)
                parts.append(split(value))
            update = dot(w_p[...], planes_rhs(parts))
            for q, x in enumerate(xs):
                step = update[0:ROWS, q * L : (q + 1) * L].reshape(NV, WL, L)
                value = plane3(x) + step * rates[x, 1][None]
                if last:
                    adj_out[:, x] = value
                else:
                    for j in range(NV):
                        ar[at(j, x), :] = value[j]
                    store_split(x, value.reshape(ROWS, L))

    pack(0)
    pl.semaphore_wait(
        barrier,
        2
        + (st > 0).astype(jnp.int32)
        + (st < n_st - 1).astype(jnp.int32)
        + (wl > 0).astype(jnp.int32)
        + (wl < n_wl - 1).astype(jnp.int32),
    )
    send(0)

    @pl.when(at_wall)
    def _():
        for c in code_loads:
            c.wait()
        tg[...] = jnp.zeros((8, NV), F32)
        tg[0:4, :] = table[...]
        tg[4:5, :] = gain[...]
        own = (iota((ROWS, NV), 0) == WL * iota((ROWS, NV), 1)).astype(F32)
        coef = lax.dot_general(own, tg[...], (((1,), (1,)), ((), ())), precision=HI, preferred_element_type=F32)

        def coef_of(x, _):
            codes = jnp.broadcast_to(code[pl.ds(x + off, 1), :], (8, L))
            spall = jnp.broadcast_to(mask[pl.ds(x + off, 1), :], (8, L))
            hot = jnp.where(sub < 4, (codes == sub).astype(F32), jnp.where(sub == 4, spall.astype(F32), 0.0))
            wall = lax.dot_general(coef, hot, (((1,), (0,)), ((), ())), precision=HI, preferred_element_type=F32)
            diag[:, x] = one(R1, x)[None] * wall.reshape(NV, WL, L)
            return 0

        lax.fori_loop(0, X, coef_of, 0)

    loads[3].wait()
    local()
    receive(0)
    finish(0, False)
    pack(1)
    send(1)
    local()
    receive(1)
    finish(1, True)
    for r in range(2):
        for n, c in enumerate(copies(r)):
            when(ways[n][1], c.wait_send)


def on_device(adj_init, adj_source, velocity, sound, face_couple, precond_inv, wall_code, spall_mask, wall_table, spall_gain):
    field = jax.ShapeDtypeStruct((NV, X, WL, L), F32)
    hbm = pl.BlockSpec(memory_space=pltpu.HBM)
    inside = pl.BlockSpec(memory_space=pltpu.VMEM)
    return pl.pallas_call(
        kernel,
        out_shape=(field, field),
        in_specs=[hbm] * 10,
        out_specs=(inside, inside),
        scratch_shapes=[
            pltpu.VMEM((20 * X * WL, L), F32),
            pltpu.VMEM((NV, X, WL, L), F32),
            pltpu.VMEM((3, X, WL, L), F32),
            pltpu.VMEM((X, WL, L), F32),
            pltpu.VMEM((16, L), jnp.int32),
            pltpu.VMEM((16, L), jnp.int32),
            pltpu.VMEM((3, NV, 2, NV), F32),
            pltpu.VMEM((NV, NV), F32),
            pltpu.VMEM((4, NV), F32),
            pltpu.VMEM((1, NV), F32),
            pltpu.VMEM((NV, X, WL, L), F32),
            pltpu.VMEM((X, 2, B1, L), BF),
            pltpu.VMEM((PAIRS + 2, 6 * ROWS, 2 * L), F32),
            pltpu.VMEM((NV, X, WL, L), F32),
            pltpu.VMEM((6 * ROWS, 512), BF),
            pltpu.VMEM((B1, 512), BF),
            pltpu.VMEM((B1, 1536), BF),
            pltpu.VMEM((B1, 256), BF),
            pltpu.VMEM((32, 256 * X), BF),
            pltpu.VMEM((8, NV), F32),
            pltpu.VMEM((2, 2, 18, WL, L), F32),
            pltpu.VMEM((2, 2, WROWS, L), F32),
            pltpu.VMEM((2, 2, 2, 16, L), F32),
            pltpu.VMEM((2, 2, 18, WL, L), F32),
            pltpu.VMEM((2, 2, 24 * X, L), F32),
            pltpu.VMEM((2, 2, 2, 16, L), F32),
            pltpu.VMEM((2, 2, 32, L), F32),
            pltpu.VMEM((X, 4, WL, L), F32),
            pltpu.SemaphoreType.DMA((10,)),
            pltpu.SemaphoreType.DMA((2, 6)),
            pltpu.SemaphoreType.DMA((2, 6)),
        ],
        compiler_params=pltpu.CompilerParams(collective_id=0, has_side_effects=True, vmem_limit_bytes=67000000),
        name="sweeps",
    )(
        adj_init.reshape(NV * X * WL, L),
        adj_source,
        velocity,
        sound,
        wall_code,
        spall_mask,
        face_couple.transpose(0, 2, 1, 3),
        precond_inv,
        wall_table,
        spall_gain.reshape(1, NV),
    )


def solution(mesh):
    field = P(None, "stream", "wall", "span")
    return jax.shard_map(
        on_device,
        mesh=mesh,
        in_specs=(field, field, field, P("stream", "wall", "span"), P(), P(), P(), P(), P(), P()),
        out_specs=(field, field),
        check_vma=False,
    )
```

profile of v0, /device:TPU:16, one launch (start us, length us, event | category | flops | bytes accessed | tf_op | source)
XLA Modules:
  0.0 33.5 jit_solution(16793036336578675642)
XLA Ops:
  0.6 29.7 %sweeps.1 = (f32[17,12,8,128]{3,2,1,0:T(8,128)}, f32[17,12,8,128]{3,2,1,0:T(8,128)}) custom-call(f32[1632,128]{1,0:T(8,128)} %bitcast.3, f32[17,12,8,128]{3,2,1,0:T(8,128)} %src_in.1, f32[3,12,8,128]{3,2,1,0:T(8,128)} %vel_in.1, f32[12,8,128]{2,1,0:T(8,128)} %snd_in.1, s32[48,1024]{1,0:T(8,128)} %code_in.1, s32[48,1024]{1,0:T(8,128)} %mask_in.1, ...), custom_call_target="tpu_custom_call" | custom-call | tf_op jit(solution)/shard_map/sweeps/pallas_call | solution.py:432
  30.4 0.0 copy-start
  30.4 2.2 %copy.14 = f32[17,12,8,128]{3,2,1,0:T(8,128)} copy(f32[17,12,8,128]{3,2,1,0:T(8,128)} %get-tuple-element.4) | data formatting | bytes 1671168
  32.6 0.0 copy-done
  32.6 0.9 %copy.15 = f32[17,12,8,128]{3,2,1,0:T(8,128)} copy(f32[17,12,8,128]{3,2,1,0:T(8,128)S(1)} %copy-done) | data formatting | bytes 1671168
Async XLA Ops:
  30.4 2.2 %copy-start = (f32[17,12,8,128]{3,2,1,0:T(8,128)S(1)}, f32[17,12,8,128]{3,2,1,0:T(8,128)}, u32[]{:S(2)}) copy-start(f32[17,12,8,128]{3,2,1,0:T(8,128)} %get-tuple-element.5) | copy-start | bytes 2506756
where the time goes:
time: 33.6 us; the launch traced here: 33.5 us
  Pallas kernels  29.7 us (88%)
  local copies, waits for them, and re-layouts  3.08 us (9%)
  between operations  0.65 us (2%)
    pallas_call x1, Pallas kernels, on_device(): pl.pallas_call(kernel, out_shape=(field, field), in_specs=[hbm] * 10, out...  29.7 us
    unnamed x4, local copies, waits for them, and re-layouts  3.08 us

commit v1 on v0

--- a/solution.py
+++ b/solution.py
@@ -42,69 +42,63 @@
     return jnp.concatenate(parts + [jnp.zeros((short, hi.shape[1]), BF)], axis=0)
 
 
-def hi_lo(weights, from_lo):
-    hi = weights.astype(BF).astype(F32)
-    return jnp.where(from_lo, weights - hi, hi).astype(BF)
-
-
 def build_weights(fc, pinv, w_all, w_p, w_span, w_wall):
-    spread = (iota((B1, NV), 0) // WL == iota((B1, NV), 1)).astype(F32)
-
-    def rows_of(couple):
-        return lax.dot_general(spread, couple, (((1,), (1,)), ((), ())), precision=HI, preferred_element_type=F32)
+    spread = (iota((B1, NV), 0) // WL == iota((B1, NV), 1)).astype(BF)
+    both = [jnp.concatenate(split(fc[d].reshape(2 * NV, NV)), axis=0) for d in range(3)]
+    rows = [dot_nt(spread, v).astype(BF) for v in both]
+    p_rows = jnp.concatenate([dot(spread, v).astype(BF) for v in split(pinv[...])], axis=1)
+
+    def fold(k, length):
+        return jnp.where(k >= 2 * length, k - 2 * length, jnp.where(k >= length, k - length, k))
+
+    def picker(n_rows, width, length, s, low_at):
+        js, k = iota((2 * n_rows, width), 0), iota((2 * n_rows, width), 1)
+        low = js >= n_rows
+        js = jnp.where(low, js - n_rows, js)
+        kk = fold(k, length) if length else k
+        if s is None:
+            return js, k, kk, low == (k >= low_at)
+        return js // 2, k, kk, (low == (k >= low_at)) & (js % 2 == s)
 
     k = iota((B1, 512), 1)
-    kk = jnp.where(k >= 2 * B1, k - 2 * B1, jnp.where(k >= B1, k - B1, k))
-    used = k < 3 * B1
-    kj = iota((2 * NV, 512), 1)
-    kj = jnp.where(kj >= 2 * B1, kj - 2 * B1, jnp.where(kj >= B1, kj - B1, kj))
-    js = iota((2 * NV, 512), 0)
-    lanes = [((kj // WL == js // 2) & (js % 2 == s)).astype(F32) for s in range(2)]
-    p_lanes = (kj[:NV] // WL == js[:NV]).astype(F32)
     w = iota((B1, 512), 0) % WL
-    wk = kk % WL
-
-    def expand(rows, lanes, shift):
-        full = lax.dot_general(rows, lanes, (((1,), (0,)), ((), ())), precision=HI, preferred_element_type=F32)
-        full = jnp.where(used & (wk == w + shift), full, 0.0)
-        hi = full.astype(BF).astype(F32)
-        return jnp.where(k >= 2 * B1, full - hi, hi)
-
-    rows = [rows_of(fc[d].reshape(2 * NV, NV)) for d in range(3)]
+    wk = fold(k, B1) % WL
+
+    def expand(values, pick, shift):
+        return jnp.where(wk == w + shift, dot(values, pick), 0.0)
+
+    picks = []
+    for s in range(2):
+        j, kc, kk, ok = picker(2 * NV, 512, B1, s, 2 * B1)
+        picks.append((ok & (kk // WL == j) & (kc < 3 * B1)).astype(BF))
     for d in range(3):
         shifts = (-1, 1) if d == 1 else (0, 0)
-        both = [expand(rows[d], lanes[s], shifts[s])[:ROWS] for s in range(2)]
-        w_all[2 * ROWS * d : 2 * ROWS * (d + 1), :] = jnp.concatenate(both, axis=0).astype(BF)
-    p_rows = lax.dot_general(spread, pinv[...], (((1,), (0,)), ((), ())), precision=HI, preferred_element_type=F32)
-    w_p[...] = expand(p_rows, p_lanes, 0).astype(BF)
-
-    ks = iota((B1, 256), 1)
-    rs = iota((B1, 256), 0)
-    js = iota((2 * NV, 256), 0)
-    kj = iota((2 * NV, 256), 1)
+        pair = [expand(rows[d], picks[s], shifts[s])[:ROWS] for s in range(2)]
+        w_all[2 * ROWS * d : 2 * ROWS * (d + 1), :] = jnp.concatenate(pair, axis=0).astype(BF)
+    j, kc, kk, ok = picker(NV, 512, B1, None, 2 * B1)
+    p_pick = (ok & (kk // WL == j) & (kc < 3 * B1)).astype(BF)
+    w_p[...] = expand(p_rows, p_pick, 0).astype(BF)
+
+    ks = iota((B1, 512), 1)
+    rs = iota((B1, 512), 0)
+    low_half = ks >= 256
+    kq = jnp.where(low_half, ks - 256, ks)
     for s in range(2):
-        s_lanes = ((kj // WL == js // 2) & (js % 2 == s)).astype(F32)
-        full = lax.dot_general(rows[2], s_lanes, (((1,), (0,)), ((), ())), precision=HI, preferred_element_type=F32)
-        full = jnp.where((rs % WL == ks % WL) & (ks < ROWS), full, 0.0)
-        full = jnp.where((rs >= ROWS) & (rs == ks), 1.0, full)
-        hi = full.astype(BF)
-        lo = (full - hi.astype(F32)).astype(BF)
-        w_span[:, 768 * s : 768 * s + 256] = hi
-        w_span[:, 768 * s + 256 : 768 * s + 512] = hi
-        w_span[:, 768 * s + 512 : 768 * s + 768] = lo
-
-    def mod48(v):
-        return jnp.where(v >= 96, v - 96, jnp.where(v >= 48, v - 48, v))
-
-    kw = mod48(ks)
-    kv = mod48(kj)
+        j, kc, kk, ok = picker(2 * NV, 512, 0, s, 256)
+        kk = jnp.where(kc >= 256, kc - 256, kc)
+        full = dot(rows[2], (ok & (kk // WL == j)).astype(BF))
+        full = jnp.where((rs % WL == kq % WL) & (kq < ROWS), full, 0.0)
+        full = jnp.where((rs >= ROWS) & (rs == ks), 1.0, full).astype(BF)
+        w_span[:, 768 * s : 768 * s + 256] = full[:, 0:256]
+        w_span[:, 768 * s + 256 : 768 * s + 768] = full
+
+    ks, rs = iota((B1, 256), 1), iota((B1, 256), 0)
     full = 0.0
     for s in range(2):
-        pick = ((kv - 24 * s == js // 2) & (js % 2 == s)).astype(F32)
-        part = lax.dot_general(rows[1], pick, (((1,), (0,)), ((), ())), precision=HI, preferred_element_type=F32)
+        j, kc, kk, ok = picker(2 * NV, 256, 48, s, 96)
+        part = dot(rows[1], (ok & (kk - 24 * s == j) & (kc < 144)).astype(BF))
         full = full + jnp.where(rs % WL == (WL - 1) * s, part, 0.0)
-    full = jnp.where((ks < 144) & (rs < ROWS), full, 0.0)
-    w_wall[...] = hi_lo(full, ks >= 96)
+    w_wall[...] = jnp.where(rs < ROWS, full, 0.0).astype(BF)
 
 
 def kernel(
@@ -184,10 +178,6 @@
     t_row, t_col = iota((32, 256 * X), 0), iota((32, 256 * X), 1)
     take_at = jnp.where(t_row < 16, L - 1, 0) + L * lax.rem(t_col // L, 2)
     take[...] = ((t_col // 256 == t_row % 16) & (t_col % 256 == take_at)).astype(BF)
-    for c in small:
-        c.wait()
-    build_weights(fc, pinv, w_all, w_p, w_span, w_wall)
-
     for c in loads[:3]:
         c.wait()
     for d, slot in ((0, R0), (1, R1), (2, R2)):
@@ -390,6 +380,9 @@
         + (wl < n_wl - 1).astype(jnp.int32),
     )
     send(0)
+    for c in small:
+        c.wait()
+    build_weights(fc, pinv, w_all, w_p, w_span, w_wall)
 
     @pl.when(at_wall)
     def _():
@@ -425,11 +418,19 @@
             when(ways[n][1], c.wait_send)
 
 
+def drain(adj, res, adj_out, res_out, sem):
+    copies = [pltpu.make_async_copy(adj, adj_out, sem.at[0]), pltpu.make_async_copy(res, res_out, sem.at[1])]
+    for c in copies:
+        c.start()
+    for c in copies:
+        c.wait()
+
+
 def on_device(adj_init, adj_source, velocity, sound, face_couple, precond_inv, wall_code, spall_mask, wall_table, spall_gain):
     field = jax.ShapeDtypeStruct((NV, X, WL, L), F32)
     hbm = pl.BlockSpec(memory_space=pltpu.HBM)
     inside = pl.BlockSpec(memory_space=pltpu.VMEM)
-    return pl.pallas_call(
+    results = pl.pallas_call(
         kernel,
         out_shape=(field, field),
         in_specs=[hbm] * 10,
@@ -467,20 +468,34 @@
             pltpu.SemaphoreType.DMA((2, 6)),
             pltpu.SemaphoreType.DMA((2, 6)),
         ],
-        compiler_params=pltpu.CompilerParams(collective_id=0, has_side_effects=True, vmem_limit_bytes=67000000),
+        compiler_params=pltpu.CompilerParams(collective_id=0, has_side_effects=True, vmem_limit_bytes=40 * 1024 * 1024),
         name="sweeps",
     )(
-        adj_init.reshape(NV * X * WL, L),
-        adj_source,
-        velocity,
-        sound,
-        wall_code,
-        spall_mask,
-        face_couple.transpose(0, 2, 1, 3),
-        precond_inv,
-        wall_table,
-        spall_gain.reshape(1, NV),
+        *[
+            pltpu.with_memory_space_constraint(v, pltpu.HBM)
+            for v in (
+                adj_init.reshape(NV * X * WL, L),
+                adj_source,
+                velocity,
+                sound,
+                wall_code,
+                spall_mask,
+                face_couple.transpose(0, 2, 1, 3),
+                precond_inv,
+                wall_table,
+                spall_gain.reshape(1, NV),
+            )
+        ]
     )
+    return pl.pallas_call(
+        drain,
+        out_shape=(field, field),
+        in_specs=[inside] * 2,
+        out_specs=(hbm, hbm),
+        scratch_shapes=[pltpu.SemaphoreType.DMA((2,))],
+        compiler_params=pltpu.CompilerParams(vmem_limit_bytes=40 * 1024 * 1024),
+        name="drain",
+    )(*results)
 
 
 def solution(mesh):

time: 33.6 us -> 30.7 us (0.914)
  the two profiles are of different devices: /device:TPU:16 before, /device:TPU:32 now
where the time goes in v1:
time: 30.7 us; the launch traced here: 30.6 us
  Pallas kernels  29.9 us (97%)
  between operations  0.64 us (2%)
    pallas_call x1, Pallas kernels, on_device(): pl.pallas_call(kernel, out_shape=(field, field), in_specs=[hbm] * 10, out...  28.7 us
    pallas_call x1, Pallas kernels, on_device(): pl.pallas_call(drain, out_shape=(field, field), in_specs=[inside] * 2, ou...  1.19 us

profile of v1, /device:TPU:32, one launch (start us, length us, event | category | flops | bytes accessed | tf_op | source)
XLA Modules:
  0.0 30.6 jit_solution(9099353057770163777)
XLA Ops:
  0.6 28.7 %sweeps.1 = (f32[17,12,8,128]{3,2,1,0:T(8,128)S(1)}, f32[17,12,8,128]{3,2,1,0:T(8,128)S(1)}) custom-call(f32[1632,128]{1,0:T(8,128)} %bitcast.3, f32[17,12,8,128]{3,2,1,0:T(8,128)} %src_in.1, f32[3,12,8,128]{3,2,1,0:T(8,128)} %vel_in.1, f32[12,8,128]{2,1,0:T(8,128)} %snd_in.1, s32[48,1024]{1,0:T(8,128)} %code_in.1, s32[48,1024]{1,0:T(8,128)} %mask_in.1, ...), custom_call_target="tpu_custom_call" | custom-call | tf_op jit(solution)/shard_map/sweeps/pallas_call | solution.py:433
  29.4 1.2 %drain.1 = (f32[17,12,8,128]{3,2,1,0:T(8,128)}, f32[17,12,8,128]{3,2,1,0:T(8,128)}) custom-call(f32[17,12,8,128]{3,2,1,0:T(8,128)S(1)} %get-tuple-element.4.adj, f32[17,12,8,128]{3,2,1,0:T(8,128)S(1)} %get-tuple-element.5.res), custom_call_target="tpu_custom_call" | custom-call | tf_op jit(solution)/shard_map/drain/pallas_call | solution.py:490

commit v2 on v1

--- a/solution.py
+++ b/solution.py
@@ -81,13 +81,14 @@
 
     ks = iota((B1, 512), 1)
     rs = iota((B1, 512), 0)
-    low_half = ks >= 256
-    kq = jnp.where(low_half, ks - 256, ks)
+    kq = jnp.where(ks >= 256, ks - 256, ks)
+    same_cell = (rs % WL == kq % WL) & (kq < ROWS)
+
     for s in range(2):
-        j, kc, kk, ok = picker(2 * NV, 512, 0, s, 256)
+        j, kc, _, ok = picker(2 * NV, 512, 0, s, 256)
         kk = jnp.where(kc >= 256, kc - 256, kc)
         full = dot(rows[2], (ok & (kk // WL == j)).astype(BF))
-        full = jnp.where((rs % WL == kq % WL) & (kq < ROWS), full, 0.0)
+        full = jnp.where(same_cell, full, 0.0)
         full = jnp.where((rs >= ROWS) & (rs == ks), 1.0, full).astype(BF)
         w_span[:, 768 * s : 768 * s + 256] = full[:, 0:256]
         w_span[:, 768 * s + 256 : 768 * s + 768] = full
@@ -103,10 +104,10 @@
 
 def kernel(
     adj_in, src_in, vel_in, snd_in, code_in, mask_in, fc_in, pinv_in, table_in, gain_in,
-    adj_out, res_out,
+    adj_out, res_out, t_adj, t_res,
     ar, src, vel, snd, code, mask, fc, pinv, table, gain, res, split_a, g_buf, diag,
-    w_all, w_p, w_span, w_wall, take, tg,
-    send_s, send_w, send_p, recv_s, recv_w, recv_p, spread, rates,
+    w_all, w_p, w_span, w_wall, tg,
+    send_s, send_w, send_p, recv_s, recv_w, recv_p, spread, rates, cols, col_rates,
     in_sem, send_sem, recv_sem,
 ):
     st, sp, wl = (lax.axis_index(a) for a in ("stream", "span", "wall"))
@@ -162,7 +163,6 @@
     for r in range(2):
         for side in range(2):
             recv_w[r, side, WROWS:, :] = jnp.zeros((recv_w.shape[2] - WROWS, L), F32)
-            spread[side] = jnp.zeros((2, 32, L), F32)
             send_p[r, side] = jnp.zeros((2, 16, L), F32)
 
             @pl.when(jnp.logical_not(ways[side][2]))
@@ -173,11 +173,13 @@
             def _():
                 recv_w[r, side, 0:WROWS, :] = jnp.zeros((WROWS, L), F32)
 
+    spread[...] = jnp.zeros((2, 2, 32, L), F32)
     g_buf[0, 0:ROWS, :] = jnp.zeros((ROWS, 2 * L), F32)
     g_buf[PAIRS + 1, ROWS : 2 * ROWS, :] = jnp.zeros((ROWS, 2 * L), F32)
-    t_row, t_col = iota((32, 256 * X), 0), iota((32, 256 * X), 1)
-    take_at = jnp.where(t_row < 16, L - 1, 0) + L * lax.rem(t_col // L, 2)
-    take[...] = ((t_col // 256 == t_row % 16) & (t_col % 256 == take_at)).astype(BF)
+    for c in small:
+        c.wait()
+    build_weights(fc, pinv, w_all, w_p, w_span, w_wall)
+
     for c in loads[:3]:
         c.wait()
     for d, slot in ((0, R0), (1, R1), (2, R2)):
@@ -196,20 +198,15 @@
     def plane3(x):
         return plane(x).reshape(NV, WL, L)
 
-    def store_split(x, value):
-        hi, lo = split(jnp.concatenate([value, one(R2, x)], axis=0))
+    def store_split(x, value, extra):
+        hi, lo = split(jnp.concatenate([value, extra], axis=0))
         split_a[x, 0] = hi
         split_a[x, 1] = lo
 
-    def first_split(x, _):
-        store_split(x, plane(x))
-        return 0
-
-    lax.fori_loop(0, X, first_split, 0)
-
-    def copies(r):
+    def copies(r, which):
         out = []
-        for n, (device, _, _) in enumerate(ways):
+        for n in which:
+            device = ways[n][0]
             bufs = ((send_s, recv_s), (send_w, recv_w), (send_p, recv_p))[n // 2]
             side = n % 2
             if n // 2 == 1:
@@ -228,28 +225,43 @@
             )
         return out
 
+    lanes3 = iota((B1, L), 1)
+    pick_row, pick_col = iota((32, 2 * L), 0), iota((32, 2 * L), 1) % L
+    pick_col = jnp.where(pick_row < 16, pick_col - 2 * pick_row - 1, pick_col - 2 * (pick_row - 16) - 2)
+    pick_cols = ((pick_col == 0) & (pick_row % 16 < X)).astype(BF)
+
+    def collect(x, value, into):
+        moved = pltpu.roll(value, 2 * x + 2, 1)
+        return jnp.where((lanes3 == 2 * x + 1) | (lanes3 == 2 * x + 2), moved, into)
+
+    def to_rows(value):
+        return dot_nt(pick_cols, jnp.concatenate(split(value), axis=1))
+
+    def put_columns(r, value):
+        for side in range(2):
+            send_p[r, side, 0] = value[16 * side : 16 * side + 16, 0:L]
+            send_p[r, side, 1, :, 0 : B1 - L] = value[16 * side : 16 * side + 16, L:B1]
+
     def pack(r):
-        faces = jnp.concatenate([split_a[x, h] for x in range(X) for h in range(2)], axis=1)
-        both = dot_nt(take[...], faces)
-        for side in range(2):
-            send_p[r, side, 0] = both[16 * side : 16 * side + 16, 0:L]
-            send_p[r, side, 1, :, 0 : B1 - L] = both[16 * side : 16 * side + 16, L:B1]
         for side, w in ((0, WL - 1), (1, 0)):
             send_w[r, side] = ar[pl.ds(w, WROWS, stride=WL), :]
         for side, x in ((0, X - 1), (1, 0)):
             send_s[r, side, 0:NV] = plane3(x)
             send_s[r, side, NV] = one(R0, x)
 
-    def send(r):
-        for n, c in enumerate(copies(r)):
+    near, far = range(4), range(4, 6)
+
+    def send(r, which):
+        for n, c in zip(which, copies(r, which)):
             when(ways[n][1], c.start)
 
-    def receive(r):
-        for n, c in enumerate(copies(r)):
+    def receive(r, which):
+        for n, c in zip(which, copies(r, which)):
             when(ways[n][2], c.wait_recv)
 
     lane = iota((WL, L), 1)
     sub = iota((WL, L), 0)
+    edge_lane = (lane == 0) | (lane == L - 1)
 
     def planes_rhs(hi_lo_pairs):
         return jnp.concatenate([stacked(h, l, 512) for h, l in hi_lo_pairs], axis=1)
@@ -305,17 +317,6 @@
             lax.fori_loop(0, X, wall_term, 0)
 
     def finish(r, last):
-        for side in range(2):
-            for half in range(2):
-                spread[side, half, pl.ds(2 - side, X, stride=2), :] = recv_p[r, side, half, 0:X, :]
-        cols = []
-        for side in range(2):
-            hi, lo = split(jnp.concatenate([spread[side, 0], spread[side, 1]], axis=1))
-            cols += [hi, lo, hi]
-        cols = jnp.concatenate(cols, axis=1)
-        cols = jnp.concatenate([cols, jnp.zeros((L - 32, cols.shape[1]), BF)], axis=0)
-        edge_cols = dot_nt(w_span[...], cols)
-
         ends = [split(recv_s[r, side].reshape(B1, L)) for side in range(2)]
         g_ends = dot(w_all[0 : 2 * ROWS, :], planes_rhs(ends))
         for side, x in ((0, 0), (1, X - 1)):
@@ -323,6 +324,7 @@
             g_end = g_ends[side * ROWS : (side + 1) * ROWS, side * L : (side + 1) * L]
             res[:, x] = res[:, x] - rate[None] * g_end.reshape(NV, WL, L)
 
+        columns = jnp.zeros((B1, L), F32)
         for p in range(PAIRS):
             xs = (2 * p, 2 * p + 1)
             rhs = []
@@ -332,7 +334,6 @@
             g_wall = dot(w_wall[...], jnp.concatenate(rhs, axis=1))
             parts = []
             for q, x in enumerate(xs):
-                edge = pltpu.roll(edge_cols, (2 * L - 2 * x - 2) % L, 1)
                 if r == 0:
                     r0, r1, r2 = one(R0, x), one(R1, x), one(R2, x)
                     r0m = recv_s[r, 0, NV] if x == 0 else one(R0, x - 1)
@@ -341,20 +342,15 @@
                     high = recv_w[r, 1, NV * X + x : NV * X + x + 1, :]
                     r1m = jnp.where(sub == 0, jnp.broadcast_to(low, (WL, L)), pltpu.roll(r1, 1, 0))
                     r1p = jnp.where(sub == WL - 1, jnp.broadcast_to(high, (WL, L)), pltpu.roll(r1, WL - 1, 0))
-                    beyond = edge[ROWS:B1]
-                    r2m = jnp.where(lane == 0, beyond, pltpu.roll(r2, 1, 1))
-                    r2p = jnp.where(lane == L - 1, beyond, pltpu.roll(r2, L - 1, 1))
+                    r2m = jnp.where(lane == 0, 0.0, pltpu.roll(r2, 1, 1))
+                    r2p = jnp.where(lane == L - 1, 0.0, pltpu.roll(r2, L - 1, 1))
                     total = 1.0 + (r0 + r1 + r2) + 0.5 * ((r0m + r0p) + (r1m + r1p) + (r2m + r2p))
-                    rate_w = jnp.where(sub == 0, 0.5 * (r1 + r1m), jnp.where(sub == WL - 1, 0.5 * (r1 + r1p), 0.0))
-                    rate_s = jnp.where(lane == 0, 0.5 * (r2 + r2m), jnp.where(lane == L - 1, 0.5 * (r2 + r2p), 0.0))
                     rates[x, 0] = total
                     rates[x, 1] = 1.0 / total
-                    rates[x, 2] = rate_w
-                    rates[x, 3] = rate_s
-                total, rate_w, rate_s = rates[x, 0], rates[x, 2], rates[x, 3]
+                    rates[x, 2] = jnp.where(sub == 0, 0.5 * (r1 + r1m), jnp.where(sub == WL - 1, 0.5 * (r1 + r1p), 0.0))
+                total, rate_w = rates[x, 0], rates[x, 2]
                 value = res[:, x] - total[None] * plane3(x)
                 value = value - rate_w[None] * g_wall[0:ROWS, q * L : (q + 1) * L].reshape(NV, WL, L)
-                value = value - rate_s[None] * edge[0:ROWS].reshape(NV, WL, L)
                 if last:
                     res_out[:, x] = value
                 value = jnp.concatenate([value.reshape(ROWS, L), jnp.zeros((WL, L), F32)], axis=0)
@@ -368,8 +364,63 @@
                 else:
                     for j in range(NV):
                         ar[at(j, x), :] = value[j]
-                    store_split(x, value.reshape(ROWS, L))
-
+                    step = jnp.concatenate([step.reshape(ROWS, L), rates[x, 0]], axis=0)
+                    columns = collect(x, step, columns)
+        if not last:
+            cols[1] = columns
+
+    def edges(r):
+        halo = []
+        for side in range(2):
+            for half in range(2):
+                spread[side, half, pl.ds(2 - side, X, stride=2), :] = recv_p[r, side, half, 0:X, :]
+            hi, lo = split(jnp.concatenate([spread[side, 0], spread[side, 1]], axis=1))
+            halo += [hi, lo, hi]
+        halo = jnp.concatenate(halo, axis=1)
+        halo = jnp.concatenate([halo, jnp.zeros((L - 32, halo.shape[1]), BF)], axis=0)
+        halo = dot_nt(w_span[...], halo)
+        flow = halo[0:ROWS].reshape(NV, WL, L)
+        if r == 0:
+            beyond = halo[ROWS:B1]
+            total = cols[1, ROWS:B1, :] + 0.5 * beyond
+            rate = 0.5 * (cols[0, ROWS:B1, :] + beyond)
+            used = (lane >= 1) & (lane <= 2 * X)
+            total = jnp.where(used, total, 1.0)
+            inverse = 1.0 / total
+            col_rates[0] = rate
+            col_rates[1] = inverse
+            before = cols[0, 0:ROWS, :].reshape(NV, WL, L)
+            change = -(0.5 * beyond)[None] * before - rate[None] * flow
+        else:
+            inverse = col_rates[1]
+            change = -col_rates[0][None] * flow
+        change = jnp.concatenate([change.reshape(ROWS, L), jnp.zeros((WL, L), F32)], axis=0)
+        moved = dot(w_p[...], stacked(*split(change), 512))
+        moved = moved[0:ROWS].reshape(NV, WL, L)
+        if r == 0:
+            update = cols[1, 0:ROWS, :].reshape(NV, WL, L) + moved
+            value = before + update * inverse[None]
+            return jnp.concatenate([value.reshape(ROWS, L), total], axis=0)
+        return change, jnp.concatenate([(moved * inverse[None]).reshape(ROWS, L), jnp.zeros((WL, L), F32)], axis=0)
+
+    def apply(turned):
+        for x in range(X):
+            edge = pltpu.roll(turned, edge_turn(x), 1)
+            value = jnp.where(edge_lane[None], edge[0:ROWS].reshape(NV, WL, L), plane3(x))
+            total = jnp.where(edge_lane, edge[ROWS:B1], rates[x, 0])
+            rates[x, 0] = total
+            rates[x, 1] = 1.0 / total
+            for j in range(NV):
+                ar[at(j, x), :] = value[j]
+            store_split(x, value.reshape(ROWS, L), total)
+
+    columns = jnp.zeros((B1, L), F32)
+    for x in range(X):
+        value = plane(x)
+        store_split(x, value, one(R2, x))
+        columns = collect(x, jnp.concatenate([value, one(R2, x)], axis=0), columns)
+    put_columns(0, to_rows(columns))
+    cols[0] = columns
     pack(0)
     pl.semaphore_wait(
         barrier,
@@ -379,10 +430,8 @@
         + (wl > 0).astype(jnp.int32)
         + (wl < n_wl - 1).astype(jnp.int32),
     )
-    send(0)
-    for c in small:
-        c.wait()
-    build_weights(fc, pinv, w_all, w_p, w_span, w_wall)
+    send(0, far)
+    send(0, near)
 
     @pl.when(at_wall)
     def _():
@@ -406,35 +455,56 @@
 
     loads[3].wait()
     local()
-    receive(0)
+    receive(0, near)
     finish(0, False)
+    receive(0, far)
+    edge_adj = edges(0)
+    put_columns(1, to_rows(edge_adj))
+    send(1, far)
+    apply(edge_adj)
     pack(1)
-    send(1)
+    send(1, near)
     local()
-    receive(1)
+    receive(1, near)
     finish(1, True)
+    receive(1, far)
+    t_res[...], t_adj[...] = edges(1)
     for r in range(2):
-        for n, c in enumerate(copies(r)):
+        for n, c in enumerate(copies(r, range(6))):
             when(ways[n][1], c.wait_send)
 
 
-def drain(adj, res, adj_out, res_out, sem):
-    copies = [pltpu.make_async_copy(adj, adj_out, sem.at[0]), pltpu.make_async_copy(res, res_out, sem.at[1])]
-    for c in copies:
-        c.start()
+def edge_turn(x):
+    return (2 * L - 2 * x - 2) % L
+
+
+def drain(adj, res, t_adj, t_res, adj_out, res_out, adj_buf, res_buf, sem):
+    lane = iota((WL, L), 1)
+    edge_lane = ((lane == 0) | (lane == L - 1))[None]
+    copies = []
+    for p in range(PAIRS):
+        part = pl.ds(2 * p, 2)
+        for n, (field, turned, buf, out) in enumerate(((adj, t_adj, adj_buf, adj_out), (res, t_res, res_buf, res_out))):
+            for x in (2 * p, 2 * p + 1):
+                edge = pltpu.roll(turned[0:ROWS, :], edge_turn(x), 1).reshape(NV, WL, L)
+                buf[:, x] = field[:, x] + jnp.where(edge_lane, edge, 0.0)
+            copy = pltpu.make_async_copy(buf.at[:, part], out.at[:, part], sem.at[n, p])
+            copy.start()
+            copies.append(copy)
     for c in copies:
         c.wait()
 
 
 def on_device(adj_init, adj_source, velocity, sound, face_couple, precond_inv, wall_code, spall_mask, wall_table, spall_gain):
     field = jax.ShapeDtypeStruct((NV, X, WL, L), F32)
+    turned = jax.ShapeDtypeStruct((B1, L), F32)
     hbm = pl.BlockSpec(memory_space=pltpu.HBM)
     inside = pl.BlockSpec(memory_space=pltpu.VMEM)
     results = pl.pallas_call(
         kernel,
-        out_shape=(field, field),
+        out_shape=(field, field, turned, turned),
         in_specs=[hbm] * 10,
-        out_specs=(inside, inside),
+        out_specs=(inside,) * 4,
         scratch_shapes=[
             pltpu.VMEM((20 * X * WL, L), F32),
             pltpu.VMEM((NV, X, WL, L), F32),
@@ -454,7 +524,6 @@
             pltpu.VMEM((B1, 512), BF),
             pltpu.VMEM((B1, 1536), BF),
             pltpu.VMEM((B1, 256), BF),
-            pltpu.VMEM((32, 256 * X), BF),
             pltpu.VMEM((8, NV), F32),
             pltpu.VMEM((2, 2, 18, WL, L), F32),
             pltpu.VMEM((2, 2, WROWS, L), F32),
@@ -464,6 +533,8 @@
             pltpu.VMEM((2, 2, 2, 16, L), F32),
             pltpu.VMEM((2, 2, 32, L), F32),
             pltpu.VMEM((X, 4, WL, L), F32),
+            pltpu.VMEM((2, B1, L), F32),
+            pltpu.VMEM((2, WL, L), F32),
             pltpu.SemaphoreType.DMA((10,)),
             pltpu.SemaphoreType.DMA((2, 6)),
             pltpu.SemaphoreType.DMA((2, 6)),
@@ -490,9 +561,13 @@
     return pl.pallas_call(
         drain,
         out_shape=(field, field),
-        in_specs=[inside] * 2,
+        in_specs=[inside] * 4,
         out_specs=(hbm, hbm),
-        scratch_shapes=[pltpu.SemaphoreType.DMA((2,))],
+        scratch_shapes=[
+            pltpu.VMEM((NV, X, WL, L), F32),
+            pltpu.VMEM((NV, X, WL, L), F32),
+            pltpu.SemaphoreType.DMA((2, PAIRS)),
+        ],
         compiler_params=pltpu.CompilerParams(vmem_limit_bytes=40 * 1024 * 1024),
         name="drain",
     )(*results)

time: 30.7 us -> 28.4 us (0.925)
  the two profiles are of different devices: /device:TPU:32 before, /device:TPU:25 now
where the time goes in v2:
time: 28.4 us; the launch traced here: 28.3 us
  Pallas kernels  27.7 us (98%)
  between operations  0.64 us (2%)
    pallas_call x1, Pallas kernels, on_device(): pl.pallas_call(kernel, out_shape=(field, field, turned, turned), in_specs...  26.3 us
    pallas_call x1, Pallas kernels, on_device(): pl.pallas_call(drain, out_shape=(field, field), in_specs=[inside] * 4, ou...  1.37 us

profile of v2, /device:TPU:25, one launch (start us, length us, event | category | flops | bytes accessed | tf_op | source)
XLA Modules:
  0.0 28.3 jit_solution(9960631602981023933)
XLA Ops:
  0.6 26.3 %sweeps.1 = (f32[17,12,8,128]{3,2,1,0:T(8,128)S(1)}, f32[17,12,8,128]{3,2,1,0:T(8,128)S(1)}, f32[144,128]{1,0:T(8,128)S(1)}, f32[144,128]{1,0:T(8,128)S(1)}) custom-call(f32[1632,128]{1,0:T(8,128)} %bitcast.3, f32[17,12,8,128]{3,2,1,0:T(8,128)} %src_in.1, f32[3,12,8,128]{3,2,1,0:T(8,128)} %vel_in.1, f32[12,8,128]{2,1,0:T(8,128)} %snd_in.1, ...), custom_call_target="tpu_custom_call" | custom-call | tf_op jit(solution)/shard_map/sweeps/pallas_call | solution.py:503
  26.9 1.4 %drain.1 = (f32[17,12,8,128]{3,2,1,0:T(8,128)}, f32[17,12,8,128]{3,2,1,0:T(8,128)}) custom-call(f32[17,12,8,128]{3,2,1,0:T(8,128)S(1)} %get-tuple-element.6.adj, f32[17,12,8,128]{3,2,1,0:T(8,128)S(1)} %get-tuple-element.7.res, f32[144,128]{1,0:T(8,128)S(1)} %get-tuple-element.8.t_adj, f32[144,128]{1,0:T(8,128)S(1)} %get-tuple-element.9.t_res), custom_call_target="tpu_custom_call" | custom-call | tf_op jit(solution)/shard_map/drain/pallas_call | solution.py:561

commit v3 on v2

--- a/solution.py
+++ b/solution.py
@@ -90,8 +90,8 @@
         full = dot(rows[2], (ok & (kk // WL == j)).astype(BF))
         full = jnp.where(same_cell, full, 0.0)
         full = jnp.where((rs >= ROWS) & (rs == ks), 1.0, full).astype(BF)
-        w_span[:, 768 * s : 768 * s + 256] = full[:, 0:256]
-        w_span[:, 768 * s + 256 : 768 * s + 768] = full
+        w_span[B1 * s : B1 * (s + 1), 0:256] = full[:, 0:256]
+        w_span[B1 * s : B1 * (s + 1), 256:768] = full
 
     ks, rs = iota((B1, 256), 1), iota((B1, 256), 0)
     full = 0.0
@@ -129,7 +129,7 @@
             pl.when(cond)(fn)
 
     barrier = pltpu.get_barrier_semaphore()
-    for device, sends, _ in ways:
+    for device, sends, _ in ways[4:] + ways[:4]:
         when(sends, lambda device=device: pl.semaphore_signal(barrier, inc=1, device_id=device, device_id_type=MESH))
 
     loads = [
@@ -173,7 +173,7 @@
             def _():
                 recv_w[r, side, 0:WROWS, :] = jnp.zeros((WROWS, L), F32)
 
-    spread[...] = jnp.zeros((2, 2, 32, L), F32)
+    spread[...] = jnp.zeros((2, 32, L), F32)
     g_buf[0, 0:ROWS, :] = jnp.zeros((ROWS, 2 * L), F32)
     g_buf[PAIRS + 1, ROWS : 2 * ROWS, :] = jnp.zeros((ROWS, 2 * L), F32)
     for c in small:
@@ -270,17 +270,14 @@
         def couple(p, _):
             rhs = planes_rhs([(split_a[2 * p + q, 0], split_a[2 * p + q, 1]) for q in range(2)])
             g_buf[p + 1] = dot(w_all[...], rhs)
-            return 0
-
-        lax.fori_loop(0, PAIRS, couple, 0)
 
         def gather(p, _):
             for q in range(2):
                 x = 2 * p + q
                 here = slice(q * L, (q + 1) * L)
                 r0, r1, r2 = one(R0, x), one(R1, x), one(R2, x)
-                m00 = 0.5 * (r0 + one(R0, jnp.maximum(x - 1, 0)))
-                m01 = 0.5 * (r0 + one(R0, jnp.minimum(x + 1, X - 1)))
+                m00 = 0.5 * (r0 + one(R0, max(x - 1, 0)))
+                m01 = 0.5 * (r0 + one(R0, min(x + 1, X - 1)))
                 m10 = 0.5 * (r1 + pltpu.roll(r1, 1, 0))
                 m11 = 0.5 * (r1 + pltpu.roll(r1, WL - 1, 0))
                 m20 = jnp.where(lane == 0, 0.0, 0.5 * (r2 + pltpu.roll(r2, 1, 1)))
@@ -304,9 +301,12 @@
                 for m, v in terms:
                     total = total - m[None] * v.reshape(NV, WL, L)
                 res[:, x] = total
-            return 0
-
-        lax.fori_loop(0, PAIRS, gather, 0)
+
+        for p in range(PAIRS + 1):
+            if p < PAIRS:
+                couple(p, 0)
+            if p > 0:
+                gather(p - 1, 0)
 
         @pl.when(at_wall)
         def _():
@@ -370,15 +370,14 @@
             cols[1] = columns
 
     def edges(r):
-        halo = []
         for side in range(2):
             for half in range(2):
-                spread[side, half, pl.ds(2 - side, X, stride=2), :] = recv_p[r, side, half, 0:X, :]
-            hi, lo = split(jnp.concatenate([spread[side, 0], spread[side, 1]], axis=1))
-            halo += [hi, lo, hi]
-        halo = jnp.concatenate(halo, axis=1)
+                spread[half, pl.ds(2 - side, X, stride=2), :] = recv_p[r, side, half, 0:X, :]
+        hi, lo = split(jnp.concatenate([spread[0], spread[1]], axis=1))
+        halo = jnp.concatenate([hi, lo, hi], axis=1)
         halo = jnp.concatenate([halo, jnp.zeros((L - 32, halo.shape[1]), BF)], axis=0)
         halo = dot_nt(w_span[...], halo)
+        halo = jnp.where(lanes3 % 2 == 0, halo[0:B1], halo[B1 : 2 * B1])
         flow = halo[0:ROWS].reshape(NV, WL, L)
         if r == 0:
             beyond = halo[ROWS:B1]
@@ -441,17 +440,26 @@
         tg[0:4, :] = table[...]
         tg[4:5, :] = gain[...]
         own = (iota((ROWS, NV), 0) == WL * iota((ROWS, NV), 1)).astype(F32)
-        coef = lax.dot_general(own, tg[...], (((1,), (1,)), ((), ())), precision=HI, preferred_element_type=F32)
-
-        def coef_of(x, _):
-            codes = jnp.broadcast_to(code[pl.ds(x + off, 1), :], (8, L))
-            spall = jnp.broadcast_to(mask[pl.ds(x + off, 1), :], (8, L))
-            hot = jnp.where(sub < 4, (codes == sub).astype(F32), jnp.where(sub == 4, spall.astype(F32), 0.0))
-            wall = lax.dot_general(coef, hot, (((1,), (0,)), ((), ())), precision=HI, preferred_element_type=F32)
-            diag[:, x] = one(R1, x)[None] * wall.reshape(NV, WL, L)
+        hi, lo = split(tg[...])
+        rest = (tg[...] - hi.astype(F32) - lo.astype(F32)).astype(BF)
+        parts = jnp.concatenate([v.astype(F32) for v in (hi, lo, rest, jnp.zeros((8, NV), BF))], axis=0).astype(BF)
+        coef = dot_nt(own.astype(BF), parts).astype(BF)
+
+        def coef_of(p, _):
+            hots = []
+            for q in range(2):
+                x = 2 * p + q
+                codes = jnp.broadcast_to(code[pl.ds(x + off, 1), :], (8, L))
+                spall = jnp.broadcast_to(mask[pl.ds(x + off, 1), :], (8, L))
+                hot = jnp.where(sub < 4, (codes == sub).astype(F32), jnp.where(sub == 4, spall.astype(F32), 0.0))
+                hots.append(jnp.concatenate([hot, hot, hot, jnp.zeros((8, L), F32)], axis=0))
+            wall = dot(coef, jnp.concatenate(hots, axis=1).astype(BF))
+            for q in range(2):
+                x = 2 * p + q
+                diag[:, x] = one(R1, x)[None] * wall[:, q * L : (q + 1) * L].reshape(NV, WL, L)
             return 0
 
-        lax.fori_loop(0, X, coef_of, 0)
+        lax.fori_loop(0, PAIRS, coef_of, 0)
 
     loads[3].wait()
     local()
@@ -482,13 +490,13 @@
     lane = iota((WL, L), 1)
     edge_lane = ((lane == 0) | (lane == L - 1))[None]
     copies = []
-    for p in range(PAIRS):
-        part = pl.ds(2 * p, 2)
+    for g, (low, high) in enumerate(((0, 2), (2, 5), (5, 9), (9, 13), (13, NV))):
         for n, (field, turned, buf, out) in enumerate(((adj, t_adj, adj_buf, adj_out), (res, t_res, res_buf, res_out))):
-            for x in (2 * p, 2 * p + 1):
-                edge = pltpu.roll(turned[0:ROWS, :], edge_turn(x), 1).reshape(NV, WL, L)
-                buf[:, x] = field[:, x] + jnp.where(edge_lane, edge, 0.0)
-            copy = pltpu.make_async_copy(buf.at[:, part], out.at[:, part], sem.at[n, p])
+            part = pl.ds(low, high - low)
+            for x in range(X):
+                edge = pltpu.roll(turned[low * WL : high * WL, :], edge_turn(x), 1).reshape(high - low, WL, L)
+                buf[low:high, x] = field[low:high, x] + jnp.where(edge_lane, edge, 0.0)
+            copy = pltpu.make_async_copy(buf.at[part], out.at[part], sem.at[n, g])
             copy.start()
             copies.append(copy)
     for c in copies:
@@ -522,7 +530,7 @@
             pltpu.VMEM((NV, X, WL, L), F32),
             pltpu.VMEM((6 * ROWS, 512), BF),
             pltpu.VMEM((B1, 512), BF),
-            pltpu.VMEM((B1, 1536), BF),
+            pltpu.VMEM((2 * B1, 768), BF),
             pltpu.VMEM((B1, 256), BF),
             pltpu.VMEM((8, NV), F32),
             pltpu.VMEM((2, 2, 18, WL, L), F32),
@@ -531,7 +539,7 @@
             pltpu.VMEM((2, 2, 18, WL, L), F32),
             pltpu.VMEM((2, 2, 24 * X, L), F32),
             pltpu.VMEM((2, 2, 2, 16, L), F32),
-            pltpu.VMEM((2, 2, 32, L), F32),
+            pltpu.VMEM((2, 32, L), F32),
             pltpu.VMEM((X, 4, WL, L), F32),
             pltpu.VMEM((2, B1, L), F32),
             pltpu.VMEM((2, WL, L), F32),

time: 28.4 us -> 28.2 us (level)
  Pallas kernels: 27.7 us -> 27.4 us
where the time goes in v3:
time: 28.2 us; the launch traced here: 28.1 us
  Pallas kernels  27.4 us (97%)
  between operations  0.64 us (2%)
    pallas_call x1, Pallas kernels, on_device(): pl.pallas_call(kernel, out_shape=(field, field, turned, turned), in_specs...  26.1 us
    pallas_call x1, Pallas kernels, on_device(): pl.pallas_call(drain, out_shape=(field, field), in_specs=[inside] * 4, ou...  1.36 us

profile of v3, /device:TPU:25, one launch (start us, length us, event | category | flops | bytes accessed | tf_op | source)
XLA Modules:
  0.0 28.1 jit_solution(3421407517670590768)
XLA Ops:
  0.6 26.1 %sweeps.1 = (f32[17,12,8,128]{3,2,1,0:T(8,128)S(1)}, f32[17,12,8,128]{3,2,1,0:T(8,128)S(1)}, f32[144,128]{1,0:T(8,128)S(1)}, f32[144,128]{1,0:T(8,128)S(1)}) custom-call(f32[1632,128]{1,0:T(8,128)} %bitcast.3, f32[17,12,8,128]{3,2,1,0:T(8,128)} %src_in.1, f32[3,12,8,128]{3,2,1,0:T(8,128)} %vel_in.1, f32[12,8,128]{2,1,0:T(8,128)} %snd_in.1, ...), custom_call_target="tpu_custom_call" | custom-call | tf_op jit(solution)/shard_map/sweeps/pallas_call | solution.py:511
  26.7 1.4 %drain.1 = (f32[17,12,8,128]{3,2,1,0:T(8,128)}, f32[17,12,8,128]{3,2,1,0:T(8,128)}) custom-call(f32[17,12,8,128]{3,2,1,0:T(8,128)S(1)} %get-tuple-element.6.adj, f32[17,12,8,128]{3,2,1,0:T(8,128)S(1)} %get-tuple-element.7.res, f32[144,128]{1,0:T(8,128)S(1)} %get-tuple-element.8.t_adj, f32[144,128]{1,0:T(8,128)S(1)} %get-tuple-element.9.t_res), custom_call_target="tpu_custom_call" | custom-call | tf_op jit(solution)/shard_map/drain/pallas_call | solution.py:569

commit v4 on v3

--- a/solution.py
+++ b/solution.py
@@ -242,9 +242,11 @@
             send_p[r, side, 0] = value[16 * side : 16 * side + 16, 0:L]
             send_p[r, side, 1, :, 0 : B1 - L] = value[16 * side : 16 * side + 16, L:B1]
 
-    def pack(r):
+    def pack_wall(r):
         for side, w in ((0, WL - 1), (1, 0)):
             send_w[r, side] = ar[pl.ds(w, WROWS, stride=WL), :]
+
+    def pack_stream(r):
         for side, x in ((0, X - 1), (1, 0)):
             send_s[r, side, 0:NV] = plane3(x)
             send_s[r, side, NV] = one(R0, x)
@@ -402,8 +404,8 @@
             return jnp.concatenate([value.reshape(ROWS, L), total], axis=0)
         return change, jnp.concatenate([(moved * inverse[None]).reshape(ROWS, L), jnp.zeros((WL, L), F32)], axis=0)
 
-    def apply(turned):
-        for x in range(X):
+    def apply(turned, xs):
+        for x in xs:
             edge = pltpu.roll(turned, edge_turn(x), 1)
             value = jnp.where(edge_lane[None], edge[0:ROWS].reshape(NV, WL, L), plane3(x))
             total = jnp.where(edge_lane, edge[ROWS:B1], rates[x, 0])
@@ -420,7 +422,8 @@
         columns = collect(x, jnp.concatenate([value, one(R2, x)], axis=0), columns)
     put_columns(0, to_rows(columns))
     cols[0] = columns
-    pack(0)
+    pack_stream(0)
+    pack_wall(0)
     pl.semaphore_wait(
         barrier,
         2
@@ -469,9 +472,12 @@
     edge_adj = edges(0)
     put_columns(1, to_rows(edge_adj))
     send(1, far)
-    apply(edge_adj)
-    pack(1)
-    send(1, near)
+    apply(edge_adj, (0, X - 1))
+    pack_stream(1)
+    send(1, range(2))
+    apply(edge_adj, range(1, X - 1))
+    pack_wall(1)
+    send(1, range(2, 4))
     local()
     receive(1, near)
     finish(1, True)

time: 28.2 us -> 28.3 us (level)
  no operation moved by 1% of the time
where the time goes in v4:
time: 28.3 us; the launch traced here: 28.1 us
  Pallas kernels  27.5 us (97%)
  between operations  0.64 us (2%)
    pallas_call x1, Pallas kernels, on_device(): pl.pallas_call(kernel, out_shape=(field, field, turned, turned), in_specs...  26.1 us
    pallas_call x1, Pallas kernels, on_device(): pl.pallas_call(drain, out_shape=(field, field), in_specs=[inside] * 4, ou...  1.36 us

profile of v4, /device:TPU:25, one launch (start us, length us, event | category | flops | bytes accessed | tf_op | source)
XLA Modules:
  0.0 28.1 jit_solution(17338832772012797210)
XLA Ops:
  0.6 26.1 %sweeps.1 = (f32[17,12,8,128]{3,2,1,0:T(8,128)S(1)}, f32[17,12,8,128]{3,2,1,0:T(8,128)S(1)}, f32[144,128]{1,0:T(8,128)S(1)}, f32[144,128]{1,0:T(8,128)S(1)}) custom-call(f32[1632,128]{1,0:T(8,128)} %bitcast.3, f32[17,12,8,128]{3,2,1,0:T(8,128)} %src_in.1, f32[3,12,8,128]{3,2,1,0:T(8,128)} %vel_in.1, f32[12,8,128]{2,1,0:T(8,128)} %snd_in.1, ...), custom_call_target="tpu_custom_call" | custom-call | tf_op jit(solution)/shard_map/sweeps/pallas_call | solution.py:517
  26.8 1.4 %drain.1 = (f32[17,12,8,128]{3,2,1,0:T(8,128)}, f32[17,12,8,128]{3,2,1,0:T(8,128)}) custom-call(f32[17,12,8,128]{3,2,1,0:T(8,128)S(1)} %get-tuple-element.6.adj, f32[17,12,8,128]{3,2,1,0:T(8,128)S(1)} %get-tuple-element.7.res, f32[144,128]{1,0:T(8,128)S(1)} %get-tuple-element.8.t_adj, f32[144,128]{1,0:T(8,128)S(1)} %get-tuple-element.9.t_res), custom_call_target="tpu_custom_call" | custom-call | tf_op jit(solution)/shard_map/drain/pallas_call | solution.py:575
